TPU v7x, 32 devices: a whole 2x2x4 slice. The times are simulated.
32 devices in a mesh: rep: 8 (over z, core), shard: 4 (over y, x).
Axes of the slice: x: 2, y: 2, z: 4, core: 2. Of those that a mesh axis runs over, the one named last changes fastest.
Arguments:
- tokens: bfloat16 [4096, 1536], P(('rep', 'shard')), may hold values from -6 to 6
- cotangent: bfloat16 [4096, 1536], P(('rep', 'shard')), may hold values from -6 to 6
- lengths: int32 [8], P('rep'), may hold values from 128 to 512, as said below
- gain_one: bfloat16 [1536], P('shard'), may hold values from 0.5 to 1.5
- w_query: bfloat16 [1536, 1536], P('shard'), may hold values from -0.15625 to 0.15625
- w_key: bfloat16 [1536, 1536], P('shard'), may hold values from -0.15625 to 0.15625
- w_value: bfloat16 [1536, 1536], P('shard'), may hold values from -0.15625 to 0.15625
- w_path: bfloat16 [1536, 1536], P('shard'), may hold values from -0.15625 to 0.15625
- w_beta: bfloat16 [1536, 12], P('shard'), may hold values from -0.15625 to 0.15625
- w_out: bfloat16 [1536, 1536], P('shard'), may hold values from -0.625 to 0.625
- gain_two: bfloat16 [1536], P('shard'), may hold values from 0.5 to 1.5
- w_gate: bfloat16 [1536, 4096], P('shard'), may hold values from -0.15625 to 0.15625
- w_up: bfloat16 [1536, 4096], P('shard'), may hold values from -0.15625 to 0.15625
- w_down: bfloat16 [4096, 1536], P('shard'), may hold values from -0.09375 to 0.09375
Outputs:
- output: bfloat16 [4096, 1536], P(('rep', 'shard'))
- input_grad: bfloat16 [4096, 1536], P(('rep', 'shard'))
- grad_gain_one: float32 [1536], P('shard')
- grad_w_query: float32 [1536, 1536], P('shard')
- grad_w_key: float32 [1536, 1536], P('shard')
- grad_w_value: float32 [1536, 1536], P('shard')
- grad_w_path: float32 [1536, 1536], P('shard')
- grad_w_beta: float32 [1536, 12], P('shard')
- grad_w_out: float32 [1536, 1536], P('shard')
- grad_gain_two: float32 [1536], P('shard')
- grad_w_gate: float32 [1536, 4096], P('shard')
- grad_w_up: float32 [1536, 4096], P('shard')
- grad_w_down: float32 [4096, 1536], P('shard')
- rms_input: float32 [], replicated
- rms_attn: float32 [], replicated
- rms_feed: float32 [], replicated
Inputs may be any that keep to these rules, and one draw needn't show every extreme that they name: Sequence r fills the first lengths[r] of its 512 slots; at least one sequence fills all of them.
All inputs are finite; a program needn't handle non-finite values.
Results may differ from a plain program's by a relative error of at most 0.02.
Values may be sent and summed in bfloat16 or wider, within the bound.
No kernel may reach another device: no remote copies, remote signals or barrier semaphores. Data moves between devices by JAX's collectives and lax.ppermute only.
A program may use at most 320 MiB of HBM per device.

v0:
```python
import jax
import jax.numpy as jnp
from jax import lax
from jax.sharding import PartitionSpec as P

eps = 1e-06
highest = lax.Precision.HIGHEST


def rms_norm(value, gain_vec):
    factor = lax.rsqrt(jnp.mean(value * value, axis=-1, keepdims=True) + eps)
    return value * factor * gain_vec


def unit_rows(raw):
    return raw * lax.rsqrt(jnp.sum(raw * raw, axis=-1, keepdims=True) + eps)


def rounded(value):
    return lax.optimization_barrier(value.astype(jnp.bfloat16)).astype(jnp.float32)


def round_pass(value):
    return value + lax.stop_gradient(rounded(value) - value)


def split_heads(matrix, head_count):
    return matrix.reshape(matrix.shape[0], head_count, -1).transpose(1, 0, 2)


def join_heads(matrix):
    return matrix.transpose(1, 0, 2).reshape(matrix.shape[1], -1)


def mul_low(left, right):
    return jnp.dot(left, right, preferred_element_type=jnp.float32)


def back_mul(grad_rows, weight):
    return jnp.einsum("tg,fg->tf", grad_rows, weight, preferred_element_type=jnp.float32)


def weight_grad(left, right):
    return jnp.einsum("tf,tg->fg", left, right, preferred_element_type=jnp.float32)


def masks(block_len):
    row_ids = jnp.arange(block_len)[:, None]
    col_ids = jnp.arange(block_len)[None, :]
    return (col_ids < row_ids, col_ids <= row_ids)


def block_system(direction, beta_rate):
    block_len = direction.shape[1]
    strictly, up_to = masks(block_len)
    gram = jnp.einsum("htd,hsd->hts", direction, direction, precision=highest)
    return jnp.eye(block_len, dtype=jnp.float32)[None] + jnp.where(
        strictly[None], gram * beta_rate[:, None, :], 0.0
    )


def own_context(keyset, values, direction, beta_rate):
    system = block_system(direction, beta_rate)
    strictly, up_to = masks(keyset.shape[1])
    coupled = jnp.where(
        strictly[None], jnp.einsum("htd,hjd->htj", direction, keyset, precision=highest), 0.0
    )
    solved = jax.scipy.linalg.solve_triangular(system, coupled, lower=True, unit_diagonal=True)
    scaled_dir = direction * beta_rate[:, :, None]
    key_end = keyset - jnp.einsum("htj,htd->hjd", solved, scaled_dir, precision=highest)
    through = jax.scipy.linalg.solve_triangular(system, direction, lower=True, unit_diagonal=True)
    block_map = jnp.eye(direction.shape[2], dtype=jnp.float32)[None] - jnp.einsum(
        "htm,htn->hmn", scaled_dir, through, precision=highest
    )
    return (join_heads(key_end), join_heads(values), block_map[None])


def attend(
    queries, keyset, values, direction, beta_rate, key_far, value_far, maps_far, my_block, length
):
    head_count, block_len, head_width = queries.shape
    blocks = maps_far.shape[0]
    score_scale = head_width ** (-0.5)
    strictly, up_to = masks(block_len)
    system = block_system(direction, beta_rate)
    coupled = jnp.where(
        strictly[None], jnp.einsum("htd,hjd->htj", direction, keyset, precision=highest), 0.0
    )
    solved = jax.scipy.linalg.solve_triangular(system, coupled, lower=True, unit_diagonal=True)
    crossing = (
        jnp.where(
            up_to[None], jnp.einsum("hid,htd->hit", queries, direction, precision=highest), 0.0
        )
        * beta_rate[:, None, :]
    )
    near_scores = (
        jnp.einsum("hid,hjd->hij", queries, keyset, precision=highest)
        - jnp.einsum("hit,htj->hij", crossing, solved, precision=highest)
    ) * score_scale
    back_solved = jax.scipy.linalg.solve_triangular(
        system, crossing.transpose(0, 2, 1), lower=True, trans=1, unit_diagonal=True
    )
    moved = queries - jnp.einsum("hti,htd->hid", back_solved, direction, precision=highest)

    def advance(carried, item_pair):
        block_map, index = item_pair
        updated = jnp.einsum("hid,hde->hie", carried, block_map, precision=highest)
        return (jnp.where(index < my_block, updated, carried), carried)

    unused, reached = lax.scan(advance, moved, (maps_far, jnp.arange(blocks)), reverse=True)
    far_keys = key_far.reshape(blocks, block_len, head_count, head_width)
    far_values = value_far.reshape(blocks, block_len, head_count, head_width)
    far_scores = jnp.einsum("ehid,ejhd->ehij", reached, far_keys, precision=highest) * score_scale
    positions = jnp.arange(block_len)
    near_ok = up_to[None] & ((my_block * block_len + positions)[None, None, :] < length)
    block_ids = jnp.arange(blocks)
    far_ok = (block_ids[:, None, None, None] < my_block) & (
        (block_ids[:, None] * block_len + positions[None, :])[:, None, None, :] < length
    )
    near_masked = jnp.where(near_ok, near_scores, -1e30)
    far_masked = jnp.where(far_ok, far_scores, -1e30)
    row_max = jnp.maximum(jnp.max(near_masked, axis=2), jnp.max(far_masked, axis=(0, 3)))[
        :, :, None
    ]
    row_total = jnp.sum(jnp.where(near_ok, jnp.exp(near_masked - row_max), 0.0), axis=2) + jnp.sum(
        jnp.where(far_ok, jnp.exp(far_masked - row_max[None]), 0.0), axis=(0, 3)
    )
    log_total = row_max + jnp.log(row_total)[:, :, None]
    near_probs = round_pass(jnp.where(near_ok, jnp.exp(near_masked - log_total), 0.0))
    far_probs = round_pass(jnp.where(far_ok, jnp.exp(far_masked - log_total[None]), 0.0))
    return jnp.einsum("hij,hjd->hid", near_probs, values, precision=highest) + jnp.einsum(
        "ehij,ejhd->hid", far_probs, far_values, precision=highest
    )


def per_device(
    tokens,
    cotangent,
    lengths,
    gain_one,
    w_query,
    w_key,
    w_value,
    w_path,
    w_beta,
    w_out,
    gain_two,
    w_gate,
    w_up,
    w_down,
):
    gain_a, query_w, key_w, value_w, path_w, beta_w, out_w, gain_b, gate_w, up_w, down_w = (
        lax.all_gather(gain_one, "shard", axis=0, tiled=True),
        lax.all_gather(w_query, "shard", axis=0, tiled=True),
        lax.all_gather(w_key, "shard", axis=0, tiled=True),
        lax.all_gather(w_value, "shard", axis=0, tiled=True),
        lax.all_gather(w_path, "shard", axis=0, tiled=True),
        lax.all_gather(w_beta, "shard", axis=0, tiled=True),
        lax.all_gather(w_out, "shard", axis=0, tiled=True),
        lax.all_gather(gain_two, "shard", axis=0, tiled=True),
        lax.all_gather(w_gate, "shard", axis=0, tiled=True),
        lax.all_gather(w_up, "shard", axis=0, tiled=True),
        lax.all_gather(w_down, "shard", axis=0, tiled=True),
    )
    block_len = tokens.shape[0]
    width = tokens.shape[1]
    head_count = beta_w.shape[1]
    my_block = lax.axis_index("shard")
    length = lengths[0]
    live_mask = (my_block * block_len + jnp.arange(block_len) < length).astype(jnp.float32)[:, None]
    stream_in = tokens.astype(jnp.float32)
    normed_f, norm_pull = jax.vjp(rms_norm, stream_in, gain_a.astype(jnp.float32))
    normed = normed_f.astype(jnp.bfloat16)
    queries = split_heads(rounded(mul_low(normed, query_w)), head_count)
    keyset = split_heads(rounded(mul_low(normed, key_w)), head_count)
    values_h = split_heads(rounded(mul_low(normed, value_w)), head_count)
    raw = mul_low(normed, path_w).reshape(block_len, head_count, -1)
    direction_f, unit_pull = jax.vjp(unit_rows, raw)
    direction = rounded(direction_f).transpose(1, 0, 2)
    beta_rate = 2.0 * jax.nn.sigmoid(mul_low(normed, beta_w))
    (key_end, value_own, map_own), context_pull = jax.vjp(
        own_context, keyset, values_h, direction, beta_rate.T
    )
    key_far, value_far, maps_far = (
        lax.all_gather(key_end.astype(jnp.bfloat16), "shard", axis=0, tiled=True).astype(
            key_end.dtype
        ),
        lax.all_gather(value_own.astype(jnp.bfloat16), "shard", axis=0, tiled=True).astype(
            value_own.dtype
        ),
        lax.all_gather(map_own.astype(jnp.bfloat16), "shard", axis=0, tiled=True).astype(
            map_own.dtype
        ),
    )

    def local_attend(
        queries, keyset, values_h, direction, beta_heads, key_far, value_far, maps_far
    ):
        return attend(
            queries,
            keyset,
            values_h,
            direction,
            beta_heads,
            key_far,
            value_far,
            maps_far,
            my_block,
            length,
        )

    heads_out, attend_pull = jax.vjp(
        local_attend,
        queries,
        keyset,
        values_h,
        direction,
        beta_rate.T,
        key_far,
        value_far,
        maps_far,
    )
    mixed = join_heads(heads_out).astype(jnp.bfloat16)
    attn_out = mul_low(mixed, out_w)
    stream = stream_in + live_mask * attn_out
    normed_two_f, norm_two_pull = jax.vjp(rms_norm, stream, gain_b.astype(jnp.float32))
    normed_two = normed_two_f.astype(jnp.bfloat16)
    gate_pre = mul_low(normed_two, gate_w)
    up_pre = mul_low(normed_two, up_w)
    gate_sig = jax.nn.sigmoid(gate_pre)
    hidden = (gate_pre * gate_sig * up_pre).astype(jnp.bfloat16)
    feed_out = mul_low(hidden, down_w)
    output = (live_mask * (stream + feed_out)).astype(jnp.bfloat16)
    cot_rows = cotangent.astype(jnp.float32) * live_mask
    d_feed = cot_rows.astype(jnp.bfloat16)
    d_hidden = back_mul(d_feed, down_w)
    d_gate = (d_hidden * up_pre * gate_sig * (1.0 + gate_pre * (1.0 - gate_sig))).astype(
        jnp.bfloat16
    )
    d_up = (d_hidden * gate_pre * gate_sig).astype(jnp.bfloat16)
    d_normed_two = back_mul(d_gate, gate_w) + back_mul(d_up, up_w)
    d_stream_norm, grad_gain_b = norm_two_pull(d_normed_two)
    d_stream = cot_rows + d_stream_norm
    d_attn = (live_mask * d_stream).astype(jnp.bfloat16)
    d_mixed = split_heads(rounded(back_mul(d_attn, out_w)), head_count)
    (
        d_queries,
        d_keys_near,
        d_values_near,
        d_dir_near,
        d_beta_near,
        d_key_far,
        d_value_far,
        d_maps_far,
    ) = attend_pull(d_mixed)
    d_key_end, d_value_own, d_map_own = (
        lax.psum_scatter(
            d_key_far.astype(jnp.bfloat16), "shard", scatter_dimension=0, tiled=True
        ).astype(jnp.float32),
        lax.psum_scatter(
            d_value_far.astype(jnp.bfloat16), "shard", scatter_dimension=0, tiled=True
        ).astype(jnp.float32),
        lax.psum_scatter(
            d_maps_far.astype(jnp.bfloat16), "shard", scatter_dimension=0, tiled=True
        ).astype(jnp.float32),
    )
    d_keys_ctx, d_values_ctx, d_dir_ctx, d_beta_ctx = context_pull(
        (d_key_end, d_value_own, d_map_own)
    )
    d_query_b = join_heads(d_queries).astype(jnp.bfloat16)
    d_key_b = join_heads(d_keys_near + d_keys_ctx).astype(jnp.bfloat16)
    d_value_b = join_heads(d_values_near + d_values_ctx).astype(jnp.bfloat16)
    (d_raw,) = unit_pull((d_dir_near + d_dir_ctx).transpose(1, 0, 2))
    d_raw_b = d_raw.reshape(block_len, -1).astype(jnp.bfloat16)
    d_beta_total = (d_beta_near + d_beta_ctx).T
    d_logit_b = (d_beta_total * beta_rate * (1.0 - 0.5 * beta_rate)).astype(jnp.bfloat16)
    d_normed = (
        back_mul(d_query_b, query_w)
        + back_mul(d_key_b, key_w)
        + back_mul(d_value_b, value_w)
        + back_mul(d_raw_b, path_w)
        + back_mul(d_logit_b, beta_w)
    )
    d_stream_in, grad_gain_a = norm_pull(d_normed)
    input_grad = (d_stream_in + d_stream).astype(jnp.bfloat16)
    g_query = weight_grad(normed, d_query_b)
    g_key = weight_grad(normed, d_key_b)
    g_value = weight_grad(normed, d_value_b)
    g_path = weight_grad(normed, d_raw_b)
    g_beta = weight_grad(normed, d_logit_b)
    g_out = weight_grad(mixed, d_attn)
    g_gate = weight_grad(normed_two, d_gate)
    g_up = weight_grad(normed_two, d_up)
    g_down = weight_grad(hidden, d_feed)
    part_sums = (
        lax.psum_scatter(
            grad_gain_a.astype(jnp.bfloat16), "shard", scatter_dimension=0, tiled=True
        ).astype(jnp.float32),
        lax.psum_scatter(
            g_query.astype(jnp.bfloat16), "shard", scatter_dimension=0, tiled=True
        ).astype(jnp.float32),
        lax.psum_scatter(
            g_key.astype(jnp.bfloat16), "shard", scatter_dimension=0, tiled=True
        ).astype(jnp.float32),
        lax.psum_scatter(
            g_value.astype(jnp.bfloat16), "shard", scatter_dimension=0, tiled=True
        ).astype(jnp.float32),
        lax.psum_scatter(
            g_path.astype(jnp.bfloat16), "shard", scatter_dimension=0, tiled=True
        ).astype(jnp.float32),
        lax.psum_scatter(
            g_beta.astype(jnp.bfloat16), "shard", scatter_dimension=0, tiled=True
        ).astype(jnp.float32),
        lax.psum_scatter(
            g_out.astype(jnp.bfloat16), "shard", scatter_dimension=0, tiled=True
        ).astype(jnp.float32),
        lax.psum_scatter(
            grad_gain_b.astype(jnp.bfloat16), "shard", scatter_dimension=0, tiled=True
        ).astype(jnp.float32),
        lax.psum_scatter(
            g_gate.astype(jnp.bfloat16), "shard", scatter_dimension=0, tiled=True
        ).astype(jnp.float32),
        lax.psum_scatter(
            g_up.astype(jnp.bfloat16), "shard", scatter_dimension=0, tiled=True
        ).astype(jnp.float32),
        lax.psum_scatter(
            g_down.astype(jnp.bfloat16), "shard", scatter_dimension=0, tiled=True
        ).astype(jnp.float32),
    )
    owned = (
        lax.psum(part_sums[0].astype(jnp.bfloat16), "rep").astype(jnp.float32),
        lax.psum(part_sums[1].astype(jnp.bfloat16), "rep").astype(jnp.float32),
        lax.psum(part_sums[2].astype(jnp.bfloat16), "rep").astype(jnp.float32),
        lax.psum(part_sums[3].astype(jnp.bfloat16), "rep").astype(jnp.float32),
        lax.psum(part_sums[4].astype(jnp.bfloat16), "rep").astype(jnp.float32),
        lax.psum(part_sums[5].astype(jnp.bfloat16), "rep").astype(jnp.float32),
        lax.psum(part_sums[6].astype(jnp.bfloat16), "rep").astype(jnp.float32),
        lax.psum(part_sums[7].astype(jnp.bfloat16), "rep").astype(jnp.float32),
        lax.psum(part_sums[8].astype(jnp.bfloat16), "rep").astype(jnp.float32),
        lax.psum(part_sums[9].astype(jnp.bfloat16), "rep").astype(jnp.float32),
        lax.psum(part_sums[10].astype(jnp.bfloat16), "rep").astype(jnp.float32),
    )
    sq_input, sq_attn, sq_feed, live_total = lax.psum(
        (
            jnp.sum(live_mask * stream_in * stream_in),
            jnp.sum(live_mask * attn_out * attn_out),
            jnp.sum(live_mask * feed_out * feed_out),
            jnp.sum(live_mask),
        ),
        ("rep", "shard"),
    )
    denom = live_total * width
    return (
        output,
        input_grad,
        owned[0],
        owned[1],
        owned[2],
        owned[3],
        owned[4],
        owned[5],
        owned[6],
        owned[7],
        owned[8],
        owned[9],
        owned[10],
        jnp.sqrt(sq_input / denom),
        jnp.sqrt(sq_attn / denom),
        jnp.sqrt(sq_feed / denom),
    )


def solution(mesh):
    return jax.shard_map(
        per_device,
        mesh=mesh,
        in_specs=(
            P(("rep", "shard"), None),
            P(("rep", "shard"), None),
            P("rep"),
            P("shard"),
            P("shard", None),
            P("shard", None),
            P("shard", None),
            P("shard", None),
            P("shard", None),
            P("shard", None),
            P("shard"),
            P("shard", None),
            P("shard", None),
            P("shard", None),
        ),
        out_specs=(
            P(("rep", "shard"), None),
            P(("rep", "shard"), None),
            P("shard"),
            P("shard", None),
            P("shard", None),
            P("shard", None),
            P("shard", None),
            P("shard", None),
            P("shard", None),
            P("shard"),
            P("shard", None),
            P("shard", None),
            P("shard", None),
            P(),
            P(),
            P(),
        ),
        check_vma=False,
    )
```

profile of v0, /device:TPU:0, one launch (start us, length us, event | category | flops | bytes accessed | tf_op | source)
XLA Modules:
  0.0 1988.5 jit_solution(15971856994298718647)
XLA Ops:
  10.1 9.5 all-gather.1
  19.6 8.5 all_gather.46
  29.4 40.5 %all-gather.19.cloned.1.call-done = bf16[1536,1536]{1,0:T(8,128)(2,1)} async-done(((bf16[384,1536]{1,0:T(8,128)(2,1)}), bf16[1536,1536]{1,0:T(8,128)(2,1)}) %all-gather.19.cloned.1.call-update) | async-done | bytes 4718608 | tf_op jit(solution)/shard_map/all_gather | solution.py:157
  76.4 117.9 %custom-call.16 = f32[12,1,128,128]{2,3,1,0:T(8,128)S(1)} custom-call(f32[12,1,128,128]{3,2,1,0:T(8,128)S(1)} %add_bitcast_fusion), custom_call_target="InvertDiagBlocksLowerTriangular" | custom-call | tf_op jit(solution)/shard_map/jvp(jit(_solve_triangular))/vmap()/triangular_solve/custom-call.1 | solution.py:89
  216.0 8.1 all-gather.2
  228.1 20.2 %all-gather.15.cloned.1.call-done = bf16[1536,1536]{1,0:T(8,128)(2,1)} async-done(((bf16[384,1536]{1,0:T(8,128)(2,1)}), bf16[1536,1536]{1,0:T(8,128)(2,1)}) %all-gather.15.cloned.1.call-update) | async-done | bytes 4718608 | tf_op jit(solution)/shard_map/all_gather | solution.py:154
  263.0 18.5 all-gather.35.cloned.1.call-done
  285.0 29.7 %all-gather.21.cloned.1.call-done = bf16[512,1536]{0,1:T(8,128)(2,1)} async-done(((bf16[128,1536]{0,1:T(8,128)(2,1)}), bf16[512,1536]{0,1:T(8,128)(2,1)}) %all-gather.21.cloned.1.call-update) | async-done | bytes 1572880 | tf_op jit(solution)/shard_map/all_gather | solution.py:185
  321.8 19.7 while.31
  371.0 36.0 %all-gather.27.cloned.1.call-done = bf16[1536,1536]{1,0:T(8,128)(2,1)} async-done(((bf16[384,1536]{1,0:T(8,128)(2,1)}), bf16[1536,1536]{1,0:T(8,128)(2,1)}) %all-gather.27.cloned.1.call-update) | async-done | bytes 4718608 | tf_op jit(solution)/shard_map/all_gather | solution.py:159
  413.2 118.2 %all-gather.29.cloned.1.call-done = bf16[1536,4096]{1,0:T(8,128)(2,1)} async-done(((bf16[384,4096]{1,0:T(8,128)(2,1)}), bf16[1536,4096]{1,0:T(8,128)(2,1)}) %all-gather.29.cloned.1.call-update) | async-done | bytes 12582928 | tf_op jit(solution)/shard_map/all_gather | solution.py:161
  531.4 7.8 fusion.203
  539.3 116.4 %all-gather.31.cloned.1.call-done = bf16[1536,4096]{1,0:T(8,128)(2,1)} async-done(((bf16[384,4096]{1,0:T(8,128)(2,1)}), bf16[1536,4096]{1,0:T(8,128)(2,1)}) %all-gather.31.cloned.1.call-update) | async-done | bytes 12582928 | tf_op jit(solution)/shard_map/all_gather | solution.py:162
  663.5 116.5 %all-gather.33.cloned.1.call-done = bf16[4096,1536]{1,0:T(8,128)(2,1)} async-done(((bf16[1024,1536]{1,0:T(8,128)(2,1)}), bf16[4096,1536]{1,0:T(8,128)(2,1)}) %all-gather.33.cloned.1.call-update) | async-done | bytes 12582928 | tf_op jit(solution)/shard_map/all_gather | solution.py:163
  780.1 10.2 multiply_convert_fusion
  790.4 10.2 fusion.205
  800.7 9.7 multiply_reduce_fusion
  810.4 8.0 fusion.81
  832.8 8.0 fusion.31
  856.2 8.4 fusion.188
  864.6 41.8 %while.32 = (s32[]{:T(128)}, f32[12,128,128]{2,1,0:T(8,128)}, bf16[4,12,128,128]{3,2,1,0:T(8,128)(2,1)}, f32[4,12,128,128]{3,2,1,0:T(8,128)}, pred[4]{0:T(512)(1...) while((s32[]{:T(128)}, f32[12,128,128]{2,1,0:T(8,128)}, ...), condition=%wide.region_16.19_spmd.clone, body=%wide.region_15.18_spmd.clone.sunk | while | flops 605552640 | bytes 7869556 | solution.py:110
  1022.4 41.7 %reduce-scatter.29.cloned.1.call-done = bf16[384,1536]{1,0:T(8,128)(2,1)} async-done(((bf16[1536,1536]{1,0:T(8,128)(2,1)}), bf16[384,1536]{1,0:T(8,128)(2,1)}) %reduce-scatter.29.cloned.1.call-update) | async-done | bytes 1179664 | tf_op jit(solution)/shard_map/reduce_scatter | solution.py:314
  1064.0 60.5 %reduce-scatter.23.cloned.1.call-done = bf16[384,1536]{1,0:T(8,128)(2,1)} async-done(((bf16[1536,1536]{1,0:T(8,128)(2,1)}), bf16[384,1536]{1,0:T(8,128)(2,1)}) %reduce-scatter.23.cloned.1.call-update) | async-done | bytes 1179664 | tf_op jit(solution)/shard_map/reduce_scatter | solution.py:302
  1124.6 60.6 %reduce-scatter.25.cloned.1.call-done = bf16[384,1536]{1,0:T(8,128)(2,1)} async-done(((bf16[1536,1536]{1,0:T(8,128)(2,1)}), bf16[384,1536]{1,0:T(8,128)(2,1)}) %reduce-scatter.25.cloned.1.call-update) | async-done | bytes 1179664 | tf_op jit(solution)/shard_map/reduce_scatter | solution.py:305
  1185.1 60.1 %reduce-scatter.27.cloned.1.call-done = bf16[384,1536]{1,0:T(8,128)(2,1)} async-done(((bf16[1536,1536]{1,0:T(8,128)(2,1)}), bf16[384,1536]{1,0:T(8,128)(2,1)}) %reduce-scatter.27.cloned.1.call-update) | async-done | bytes 1179664 | tf_op jit(solution)/shard_map/reduce_scatter | solution.py:308
  1245.2 123.7 %reduce-scatter.31.cloned.1.call-done = bf16[384,4096]{1,0:T(8,128)(2,1)} async-done(((bf16[1536,4096]{1,0:T(8,128)(2,1)}), bf16[384,4096]{1,0:T(8,128)(2,1)}) %reduce-scatter.31.cloned.1.call-update) | async-done | bytes 3145744 | tf_op jit(solution)/shard_map/reduce_scatter | solution.py:320
  1368.9 123.9 %reduce-scatter.33.cloned.1.call-done = bf16[384,4096]{1,0:T(8,128)(2,1)} async-done(((bf16[1536,4096]{1,0:T(8,128)(2,1)}), bf16[384,4096]{1,0:T(8,128)(2,1)}) %reduce-scatter.33.cloned.1.call-update) | async-done | bytes 3145744 | tf_op jit(solution)/shard_map/reduce_scatter | solution.py:323
  1492.8 123.9 %reduce-scatter.35.cloned.1.call-done = bf16[1024,1536]{1,0:T(8,128)(2,1)} async-done(((bf16[4096,1536]{1,0:T(8,128)(2,1)}), bf16[1024,1536]{1,0:T(8,128)(2,1)}) %reduce-scatter.35.cloned.1.call-update) | async-done | bytes 3145744 | tf_op jit(solution)/shard_map/reduce_scatter | solution.py:326
  1633.7 40.3 %all-reduce.3 = (f32[]{:T(128)}, f32[]{:T(128)}, f32[]{:T(128)}, f32[]{:T(128)}) all-reduce(f32[]{:T(128)} %get-tuple-element.278, f32[]{:T(128)} %get-tuple-element.326, f32[]{:T(128)} %get-tuple-element.280, f32[]{:T(128)} %get-tuple-element.279), channel_id=1, replica_groups=mesh['rep'=8,'shard'=4] {'rep','shard'}, use_global_device_ids=true, to_apply=%region_52.55 | all-reduce | flops 4 | bytes 32 | tf_op jit(solution)/shard_map/psum | solution.py:343
  1674.0 10.8 all-reduce.6
  1689.7 28.2 %all-reduce.4 = (bf16[384]{0:T(512)(128)(2,1)S(1)}, bf16[384,12]{0,1:T(8,128)(2,1)S(1)}, bf16[384]{0:T(512)(128)(2,1)S(1)}) all-reduce(bf16[384]{0:T(512)(128)(2,1)S(1)} %dynamic-slice.3, bf16[384,12]{0,1:T(8,128)(2,1)S(1)} %copy.335, bf16[384]{0:T(512)(128)(2,1)S(1)} %dynamic-slice.5), channel_id=1, replica_groups=mesh['rep'=8,'shard'=4] {'rep'}, use_global_device_ids=true, to_apply=%region_29.32 | all-reduce | flops 5376 | bytes 21504 | tf_op jit(solution)/shard_map/psum | solution.py:331
  1719.6 238.0 %all-reduce.9.cloned.1.call-done = (bf16[384,1536]{1,0:T(8,128)(2,1)}, bf16[384,1536]{1,0:T(8,128)(2,1)}, bf16[384,1536]{1,0:T(8,128)(2,1)}, bf16[384,1536]{1,0:...) async-done(((bf16[384,1536]{1,0:T(8,128)(2,1)}, bf16[384,1536]{1,0:T(8,128)(2,1)}, ...) | async-done | bytes 15335440 | tf_op jit(solution)/shard_map/psum | solution.py:332
  (545 shorter events, 347.8 us)
Async XLA Ops:
  7.2 62.7 %all-gather.19.cloned.1.call-start = ((), (), s32[]{:S(2)}) async-start(), calls=%async_computation.14 | async-start | bytes 5898240 | tf_op jit(solution)/shard_map/all_gather | solution.py:157
  7.9 191.4 %all-gather.17.cloned.1.call-start = ((), (), s32[]{:S(2)}) async-start(), calls=%async_computation.13 | async-start | bytes 5898240 | tf_op jit(solution)/shard_map/all_gather | solution.py:155
  8.7 198.7 %all-gather.23.cloned.1.call-start = ((), (), s32[]{:S(2)}) async-start(), calls=%async_computation.16 | async-start | bytes 5898240 | tf_op jit(solution)/shard_map/all_gather | solution.py:156
  9.4 238.9 %all-gather.15.cloned.1.call-start = ((), (), s32[]{:S(2)}) async-start(), calls=%async_computation.12 | async-start | bytes 5898240 | tf_op jit(solution)/shard_map/all_gather | solution.py:154
  10.0 271.5 %all-gather.35.cloned.1.call-start = ((), (), s32[]{:S(2)}) async-start(), calls=%async_computation.30 | async-start | bytes 1966080 | tf_op jit(solution)/shard_map/all_gather | solution.py:191
  28.2 46.1 %copy-start.116 = (bf16[1536,12]{0,1:T(8,128)(2,1)}, bf16[1536,12]{0,1:T(8,128)(2,1)S(1)}, u32[]{:S(2)}) copy-start(bf16[1536,12]{0,1:T(8,128)(2,1)S(1)} %all_gather.46) | copy-start | bytes 110596
  29.0 170.4 %copy-start.108 = (f32[128]{0:T(128)}, f32[128]{0:T(128)S(1)}, u32[]{:S(2)}) copy-start(f32[128]{0:T(128)S(1)} %fusion.179) | copy-start | bytes 1540
  74.6 124.3 %copy-start.114 = (f32[128,12]{0,1:T(8,128)}, f32[128,12]{0,1:T(8,128)S(1)}, u32[]{:S(2)}) copy-start(f32[128,12]{0,1:T(8,128)S(1)} %multiply_reduce_fusion.7) | copy-start | bytes 18436
  194.3 60.0 %copy-start = (f32[12,1,128,128]{2,3,1,0:T(8,128)}, f32[12,1,128,128]{2,3,1,0:T(8,128)S(1)}, u32[]{:S(2)}) copy-start(f32[12,1,128,128]{2,3,1,0:T(8,128)S(1)} %custom-call.16) | copy-start | bytes 2359300
  199.0 115.6 %all-gather.21.cloned.1.call-start = ((), (), s32[]{:S(2)}) async-start(), calls=%async_computation.15 | async-start | bytes 1966080 | tf_op jit(solution)/shard_map/all_gather | solution.py:185
  203.2 57.3 %copy-start.16 = (bf16[128,1536]{0,1:T(8,128)(2,1)}, bf16[128,1536]{0,1:T(8,128)(2,1)S(1)}, u32[]{:S(2)}) copy-start(bf16[128,1536]{0,1:T(8,128)(2,1)S(1)} %copy.185) | copy-start | bytes 1179652
  204.9 53.4 %copy-start.9 = (f32[12,128,128]{2,1,0:T(8,128)}, f32[12,128,128]{2,1,0:T(8,128)S(1)}, u32[]{:S(2)}) copy-start(f32[12,128,128]{2,1,0:T(8,128)S(1)} %fusion.105) | copy-start | bytes 2359300
  207.4 143.5 %all-gather.25.cloned.1.call-start = ((), (), s32[]{:S(2)}) async-start(), calls=%async_computation.17 | async-start | bytes 1966080 | tf_op jit(solution)/shard_map/all_gather | solution.py:188
  211.4 195.7 %all-gather.27.cloned.1.call-start = ((), (), s32[]{:S(2)}) async-start(), calls=%async_computation.18 | async-start | bytes 5898240 | tf_op jit(solution)/shard_map/all_gather | solution.py:159
  212.1 319.3 %all-gather.29.cloned.1.call-start = ((), (), s32[]{:S(2)}) async-start(), calls=%async_computation.19 | async-start | bytes 15728640 | tf_op jit(solution)/shard_map/all_gather | solution.py:161
  212.9 442.8 %all-gather.31.cloned.1.call-start = ((), (), s32[]{:S(2)}) async-start(), calls=%async_computation.20 | async-start | bytes 15728640 | tf_op jit(solution)/shard_map/all_gather | solution.py:162
  213.5 566.6 %all-gather.33.cloned.1.call-start = ((), (), s32[]{:S(2)}) async-start(), calls=%async_computation.21 | async-start | bytes 15728640 | tf_op jit(solution)/shard_map/all_gather | solution.py:163
  214.2 724.2 %reduce-scatter.37.cloned.1.call-start = ((), (), s32[]{:S(2)}) async-start(), calls=%async_computation.31 | async-start | bytes 1966080
  843.5 108.3 %reduce-scatter.39.cloned.1.call-start = ((), (), s32[]{:S(2)}) async-start(), calls=%async_computation.32 | async-start | bytes 1966080
  856.0 116.3 %reduce-scatter.43.cloned.1.call-start = ((), (), s32[]{:S(2)}) async-start(), calls=%async_computation.34 | async-start | bytes 1966080
  906.5 115.9 %reduce-scatter.21.cloned.1.call-start = ((), (), s32[]{:S(2)}) async-start(), calls=%async_computation.22 | async-start | bytes 5898240 | tf_op jit(solution)/shard_map/reduce_scatter | solution.py:299
  923.5 140.5 %reduce-scatter.29.cloned.1.call-start = ((), (), s32[]{:S(2)}) async-start(), calls=%async_computation.26 | async-start | bytes 5898240 | tf_op jit(solution)/shard_map/reduce_scatter | solution.py:314
  928.4 196.2 %reduce-scatter.23.cloned.1.call-start = ((), (), s32[]{:S(2)}) async-start(), calls=%async_computation.23 | async-start | bytes 5898240 | tf_op jit(solution)/shard_map/reduce_scatter | solution.py:302
  951.7 233.4 %reduce-scatter.25.cloned.1.call-start = ((), (), s32[]{:S(2)}) async-start(), calls=%async_computation.24 | async-start | bytes 5898240 | tf_op jit(solution)/shard_map/reduce_scatter | solution.py:305
  960.9 284.3 %reduce-scatter.27.cloned.1.call-start = ((), (), s32[]{:S(2)}) async-start(), calls=%async_computation.25 | async-start | bytes 5898240 | tf_op jit(solution)/shard_map/reduce_scatter | solution.py:308
  996.8 372.2 %reduce-scatter.31.cloned.1.call-start = ((), (), s32[]{:S(2)}) async-start(), calls=%async_computation.27 | async-start | bytes 15728640 | tf_op jit(solution)/shard_map/reduce_scatter | solution.py:320
  1004.6 488.2 %reduce-scatter.33.cloned.1.call-start = ((), (), s32[]{:S(2)}) async-start(), calls=%async_computation.28 | async-start | bytes 15728640 | tf_op jit(solution)/shard_map/reduce_scatter | solution.py:323
  1012.2 604.5 %reduce-scatter.35.cloned.1.call-start = ((), (), s32[]{:S(2)}) async-start(), calls=%async_computation.29 | async-start | bytes 15728640 | tf_op jit(solution)/shard_map/reduce_scatter | solution.py:326
  1020.3 668.4 %reduce-scatter.41.cloned.1.call-start = ((), (), s32[]{:S(2)}) async-start(), calls=%async_computation.33 | async-start | bytes 491520
  1022.3 935.4 %all-reduce.9.cloned.1.call-start = ((), (), s32[]{:S(2)}) async-start(), calls=%async_computation.35 | async-start | bytes 30670848 | tf_op jit(solution)/shard_map/psum | solution.py:332
  1630.9 56.8 %copy-start.136 = (f32[128]{0:T(128)S(1)}, f32[128]{0:T(128)}, u32[]{:S(2)}) copy-start(f32[128]{0:T(128)} %copy-done.135) | copy-start | bytes 1540
  1630.9 56.8 %copy-start.23 = (f32[128,1536]{1,0:T(8,128)S(1)}, f32[128,1536]{1,0:T(8,128)}, u32[]{:S(2)}) copy-start(f32[128,1536]{1,0:T(8,128)} %copy-done.22) | copy-start | bytes 2359300
  (137 other events, 730.2 us)
Sparse Core Ops, SparseCore 0:
  9.9 60.0 all-gather.18
  71.8 58.0 all-gather.16
  131.7 57.6 all-gather.22
  191.1 57.1 all-gather.14
  250.5 30.9 all-gather.34
  283.8 30.8 all-gather.20
  317.1 30.9 all-gather.24
  349.9 57.0 all-gather.26
  408.9 122.5 all-gather.28
  533.1 122.5 all-gather.30
  657.5 122.5 all-gather.32
  843.6 30.9 reduce-scatter.36
  878.1 30.9 reduce-scatter.38
  912.5 30.9 reduce-scatter.42
  946.9 57.0 reduce-scatter.20
  1006.9 57.0 reduce-scatter.28
  1067.4 57.0 reduce-scatter.22
  1128.0 57.0 reduce-scatter.24
  1188.1 57.0 reduce-scatter.26
  1248.2 120.7 reduce-scatter.30
  1372.0 120.7 reduce-scatter.32
  1495.9 120.7 reduce-scatter.34
  1620.0 24.5 reduce-scatter.40
  1647.4 310.1 all-reduce.8
where the time goes:
time: 2000 us; the launch traced here: 1990 us
  waiting for transfers between devices  1330 us (66%)
  matrix products  278 us (14%)
  other arithmetic  163 us (8%)
  blocking collectives  105 us (5%)
  local copies, waits for them, and re-layouts  78.5 us (4%)
  between operations  24 us (1%)
    psum x1, waiting for transfers between devices, per_device(): lax.psum(part_sums[1].astype(jnp.bfloat16), 'rep').astype(jnp.float32)  238 us
    reduce_scatter x1, waiting for transfers between devices, per_device(): lax.psum_scatter(g_up.astype(jnp.bfloat16), 'shard', scatter_dimension=0,...  124 us
    reduce_scatter x1, waiting for transfers between devices, per_device(): lax.psum_scatter(g_down.astype(jnp.bfloat16), 'shard', scatter_dimension=...  124 us
    reduce_scatter x1, waiting for transfers between devices, per_device(): lax.psum_scatter(g_gate.astype(jnp.bfloat16), 'shard', scatter_dimension=...  124 us
    all_gather x1, waiting for transfers between devices, per_device(): lax.all_gather(w_gate, 'shard', axis=0, tiled=True)  118 us
    another operation x4, other arithmetic, attend(): jax.scipy.linalg.solve_triangular(system, coupled, lower=True, unit_diago...  118 us
    all_gather x1, waiting for transfers between devices, per_device(): lax.all_gather(w_down, 'shard', axis=0, tiled=True)  117 us
    all_gather x1, waiting for transfers between devices, per_device(): lax.all_gather(w_up, 'shard', axis=0, tiled=True)  116 us
  transfers between devices with their start and end apart: 24, of which 16 were waited for; matrix products, arithmetic and copies ran while one was open for 21% of the time, Pallas kernels for 0%

commit v1 on v0

--- a/solution.py
+++ b/solution.py
@@ -329,7 +329,9 @@
     )
     owned = (
         lax.psum(part_sums[0].astype(jnp.bfloat16), "rep").astype(jnp.float32),
-        lax.psum(part_sums[1].astype(jnp.bfloat16), "rep").astype(jnp.float32),
+        jnp.sum(lax.all_gather(part_sums[1].astype(jnp.bfloat16), "rep"), axis=0).astype(
+            jnp.float32
+        ),
         lax.psum(part_sums[2].astype(jnp.bfloat16), "rep").astype(jnp.float32),
         lax.psum(part_sums[3].astype(jnp.bfloat16), "rep").astype(jnp.float32),
         lax.psum(part_sums[4].astype(jnp.bfloat16), "rep").astype(jnp.float32),

time: 2000 us -> 2060 us (1.030)
  waiting for transfers between devices: 1330 us -> 1390 us
    psum x1, waiting for transfers between devices: 238 us -> 280 us  [per_device(): lax.psum(part_sums[2].astype(jnp.bfloat16), 'rep').astype(jnp.float32)]
  transfers between devices with their start and end apart: 24 -> 25, of which waited for: 16 -> 17; matrix products, arithmetic and copies ran while one was open for 21% -> 21% of each run, Pallas kernels for 0% -> 0%
where the time goes in v1:
time: 2060 us; the launch traced here: 2050 us
  waiting for transfers between devices  1390 us (67%)
  matrix products  278 us (13%)
  other arithmetic  169 us (8%)
  blocking collectives  106 us (5%)
  local copies, waits for them, and re-layouts  79.6 us (4%)
  between operations  23.7 us (1%)
    psum x1, waiting for transfers between devices, per_device(): lax.psum(part_sums[2].astype(jnp.bfloat16), 'rep').astype(jnp.float32)  280 us
    reduce_scatter x1, waiting for transfers between devices, per_device(): lax.psum_scatter(g_up.astype(jnp.bfloat16), 'shard', scatter_dimension=0,...  124 us
    reduce_scatter x1, waiting for transfers between devices, per_device(): lax.psum_scatter(g_down.astype(jnp.bfloat16), 'shard', scatter_dimension=...  124 us
    reduce_scatter x1, waiting for transfers between devices, per_device(): lax.psum_scatter(g_gate.astype(jnp.bfloat16), 'shard', scatter_dimension=...  124 us
    all_gather x1, waiting for transfers between devices, per_device(): lax.all_gather(w_gate, 'shard', axis=0, tiled=True)  118 us
    another operation x4, other arithmetic, attend(): jax.scipy.linalg.solve_triangular(system, coupled, lower=True, unit_diago...  118 us
    all_gather x1, waiting for transfers between devices, per_device(): lax.all_gather(w_down, 'shard', axis=0, tiled=True)  117 us
    all_gather x1, waiting for transfers between devices, per_device(): lax.all_gather(w_up, 'shard', axis=0, tiled=True)  116 us
  transfers between devices with their start and end apart: 25, of which 17 were waited for; matrix products, arithmetic and copies ran while one was open for 21% of the time, Pallas kernels for 0%

profile of v1, /device:TPU:0, one launch (start us, length us, event | category | flops | bytes accessed | tf_op | source)
XLA Modules:
  0.0 2053.6 jit_solution(16950922087343562289)
XLA Ops:
  10.1 9.5 all-gather.2
  19.6 8.5 all_gather.52
  29.3 40.6 %all-gather.21.cloned.1.call-done = bf16[1536,1536]{1,0:T(8,128)(2,1)} async-done(((bf16[384,1536]{1,0:T(8,128)(2,1)}), bf16[1536,1536]{1,0:T(8,128)(2,1)}) %all-gather.21.cloned.1.call-update) | async-done | bytes 4718608 | tf_op jit(solution)/shard_map/all_gather | solution.py:157
  77.1 117.9 %custom-call.16 = f32[12,1,128,128]{2,3,1,0:T(8,128)S(1)} custom-call(f32[12,1,128,128]{3,2,1,0:T(8,128)S(1)} %add_bitcast_fusion), custom_call_target="InvertDiagBlocksLowerTriangular" | custom-call | tf_op jit(solution)/shard_map/jvp(jit(_solve_triangular))/vmap()/triangular_solve/custom-call.1 | solution.py:89
  216.3 8.1 all-gather.3
  228.5 19.0 all-gather.17.cloned.1.call-done
  262.3 18.5 all-gather.37.cloned.1.call-done
  284.2 29.7 %all-gather.23.cloned.1.call-done = bf16[512,1536]{0,1:T(8,128)(2,1)} async-done(((bf16[128,1536]{0,1:T(8,128)(2,1)}), bf16[512,1536]{0,1:T(8,128)(2,1)}) %all-gather.23.cloned.1.call-update) | async-done | bytes 1572880 | tf_op jit(solution)/shard_map/all_gather | solution.py:185
  321.0 19.7 while.31
  370.3 35.9 %all-gather.29.cloned.1.call-done = bf16[1536,1536]{1,0:T(8,128)(2,1)} async-done(((bf16[384,1536]{1,0:T(8,128)(2,1)}), bf16[1536,1536]{1,0:T(8,128)(2,1)}) %all-gather.29.cloned.1.call-update) | async-done | bytes 4718608 | tf_op jit(solution)/shard_map/all_gather | solution.py:159
  412.4 118.2 %all-gather.31.cloned.1.call-done = bf16[1536,4096]{1,0:T(8,128)(2,1)} async-done(((bf16[384,4096]{1,0:T(8,128)(2,1)}), bf16[1536,4096]{1,0:T(8,128)(2,1)}) %all-gather.31.cloned.1.call-update) | async-done | bytes 12582928 | tf_op jit(solution)/shard_map/all_gather | solution.py:161
  538.4 116.4 %all-gather.33.cloned.1.call-done = bf16[1536,4096]{1,0:T(8,128)(2,1)} async-done(((bf16[384,4096]{1,0:T(8,128)(2,1)}), bf16[1536,4096]{1,0:T(8,128)(2,1)}) %all-gather.33.cloned.1.call-update) | async-done | bytes 12582928 | tf_op jit(solution)/shard_map/all_gather | solution.py:162
  662.7 116.5 %all-gather.35.cloned.1.call-done = bf16[4096,1536]{1,0:T(8,128)(2,1)} async-done(((bf16[1024,1536]{1,0:T(8,128)(2,1)}), bf16[4096,1536]{1,0:T(8,128)(2,1)}) %all-gather.35.cloned.1.call-update) | async-done | bytes 12582928 | tf_op jit(solution)/shard_map/all_gather | solution.py:163
  779.2 10.3 multiply_convert_fusion
  789.6 10.2 fusion.205
  799.8 9.7 multiply_reduce_fusion
  809.6 8.1 fusion.81
  832.0 8.0 fusion.31
  855.4 8.3 fusion.188
  863.8 41.9 %while.32 = (s32[]{:T(128)}, f32[12,128,128]{2,1,0:T(8,128)}, bf16[4,12,128,128]{3,2,1,0:T(8,128)(2,1)}, f32[4,12,128,128]{3,2,1,0:T(8,128)}, pred[4]{0:T(512)(1...) while((s32[]{:T(128)}, f32[12,128,128]{2,1,0:T(8,128)}, ...), condition=%wide.region_16.19_spmd.clone, body=%wide.region_15.18_spmd.clone.sunk | while | flops 605552640 | bytes 7869556 | solution.py:110
  1022.7 40.6 %reduce-scatter.29.cloned.1.call-done = bf16[384,1536]{1,0:T(8,128)(2,1)} async-done(((bf16[1536,1536]{1,0:T(8,128)(2,1)}), bf16[384,1536]{1,0:T(8,128)(2,1)}) %reduce-scatter.29.cloned.1.call-update) | async-done | bytes 1179664 | tf_op jit(solution)/shard_map/reduce_scatter | solution.py:314
  1063.3 60.5 %reduce-scatter.23.cloned.1.call-done = bf16[384,1536]{1,0:T(8,128)(2,1)} async-done(((bf16[1536,1536]{1,0:T(8,128)(2,1)}), bf16[384,1536]{1,0:T(8,128)(2,1)}) %reduce-scatter.23.cloned.1.call-update) | async-done | bytes 1179664 | tf_op jit(solution)/shard_map/reduce_scatter | solution.py:302
  1123.8 60.6 %reduce-scatter.25.cloned.1.call-done = bf16[384,1536]{1,0:T(8,128)(2,1)} async-done(((bf16[1536,1536]{1,0:T(8,128)(2,1)}), bf16[384,1536]{1,0:T(8,128)(2,1)}) %reduce-scatter.25.cloned.1.call-update) | async-done | bytes 1179664 | tf_op jit(solution)/shard_map/reduce_scatter | solution.py:305
  1184.4 60.1 %reduce-scatter.27.cloned.1.call-done = bf16[384,1536]{1,0:T(8,128)(2,1)} async-done(((bf16[1536,1536]{1,0:T(8,128)(2,1)}), bf16[384,1536]{1,0:T(8,128)(2,1)}) %reduce-scatter.27.cloned.1.call-update) | async-done | bytes 1179664 | tf_op jit(solution)/shard_map/reduce_scatter | solution.py:308
  1244.5 123.7 %reduce-scatter.31.cloned.1.call-done = bf16[384,4096]{1,0:T(8,128)(2,1)} async-done(((bf16[1536,4096]{1,0:T(8,128)(2,1)}), bf16[384,4096]{1,0:T(8,128)(2,1)}) %reduce-scatter.31.cloned.1.call-update) | async-done | bytes 3145744 | tf_op jit(solution)/shard_map/reduce_scatter | solution.py:320
  1368.2 123.9 %reduce-scatter.33.cloned.1.call-done = bf16[384,4096]{1,0:T(8,128)(2,1)} async-done(((bf16[1536,4096]{1,0:T(8,128)(2,1)}), bf16[384,4096]{1,0:T(8,128)(2,1)}) %reduce-scatter.33.cloned.1.call-update) | async-done | bytes 3145744 | tf_op jit(solution)/shard_map/reduce_scatter | solution.py:323
  1492.1 123.9 %reduce-scatter.35.cloned.1.call-done = bf16[1024,1536]{1,0:T(8,128)(2,1)} async-done(((bf16[4096,1536]{1,0:T(8,128)(2,1)}), bf16[1024,1536]{1,0:T(8,128)(2,1)}) %reduce-scatter.35.cloned.1.call-update) | async-done | bytes 3145744 | tf_op jit(solution)/shard_map/reduce_scatter | solution.py:326
  1632.9 42.2 %all-reduce.3 = (f32[]{:T(128)}, f32[]{:T(128)}, f32[]{:T(128)}, f32[]{:T(128)}) all-reduce(f32[]{:T(128)} %get-tuple-element.278, f32[]{:T(128)} %get-tuple-element.325, f32[]{:T(128)} %get-tuple-element.280, f32[]{:T(128)} %get-tuple-element.279), channel_id=1, replica_groups=mesh['rep'=8,'shard'=4] {'rep','shard'}, use_global_device_ids=true, to_apply=%region_52.55 | all-reduce | flops 4 | bytes 32 | tf_op jit(solution)/shard_map/psum | solution.py:345
  1675.1 10.2 all-reduce.6
  1690.2 27.3 %all-reduce.4 = (bf16[384]{0:T(512)(128)(2,1)S(1)}, bf16[384,12]{0,1:T(8,128)(2,1)S(1)}, bf16[384]{0:T(512)(128)(2,1)S(1)}) all-reduce(bf16[384]{0:T(512)(128)(2,1)S(1)} %dynamic-slice.3, bf16[384,12]{0,1:T(8,128)(2,1)S(1)} %copy.335, bf16[384]{0:T(512)(128)(2,1)S(1)} %dynamic-slice.5), channel_id=1, replica_groups=mesh['rep'=8,'shard'=4] {'rep'}, use_global_device_ids=true, to_apply=%region_29.32 | all-reduce | flops 5376 | bytes 21504 | tf_op jit(solution)/shard_map/psum | solution.py:331
  1719.3 17.6 all-gather.39.cloned.1.call-done
  1744.5 280.3 %all-reduce.9.cloned.1.call-done = (bf16[384,1536]{1,0:T(8,128)(2,1)}, bf16[384,1536]{1,0:T(8,128)(2,1)}, bf16[384,1536]{1,0:T(8,128)(2,1)}, bf16[384,1536]{1,0:...) async-done(((bf16[384,1536]{1,0:T(8,128)(2,1)}, bf16[384,1536]{1,0:T(8,128)(2,1)}, bf16[384,1536]{1,0:T(8,128)(2,1)}, ...) | async-done | bytes 14155792 | tf_op jit(solution)/shard_map/psum | solution.py:335
  (547 shorter events, 363.1 us)
Async XLA Ops:
  7.2 62.7 %all-gather.21.cloned.1.call-start = ((), (), s32[]{:S(2)}) async-start(), calls=%async_computation.14 | async-start | bytes 5898240 | tf_op jit(solution)/shard_map/all_gather | solution.py:157
  7.9 192.2 %all-gather.19.cloned.1.call-start = ((), (), s32[]{:S(2)}) async-start(), calls=%async_computation.13 | async-start | bytes 5898240 | tf_op jit(solution)/shard_map/all_gather | solution.py:155
  8.7 199.0 %all-gather.25.cloned.1.call-start = ((), (), s32[]{:S(2)}) async-start(), calls=%async_computation.16 | async-start | bytes 5898240 | tf_op jit(solution)/shard_map/all_gather | solution.py:156
  9.4 238.0 %all-gather.17.cloned.1.call-start = ((), (), s32[]{:S(2)}) async-start(), calls=%async_computation.12 | async-start | bytes 5898240 | tf_op jit(solution)/shard_map/all_gather | solution.py:154
  10.0 270.7 %all-gather.37.cloned.1.call-start = ((), (), s32[]{:S(2)}) async-start(), calls=%async_computation.30 | async-start | bytes 1966080 | tf_op jit(solution)/shard_map/all_gather | solution.py:191
  28.9 171.2 %copy-start.107 = (f32[128]{0:T(128)}, f32[128]{0:T(128)S(1)}, u32[]{:S(2)}) copy-start(f32[128]{0:T(128)S(1)} %fusion.179) | copy-start | bytes 1540
  29.3 46.8 %copy-start.83 = (pred[128,128]{1,0:T(8,128)(4,1)}, pred[128,128]{1,0:T(8,128)(4,1)S(1)}, u32[]{:S(2)}) copy-start(pred[128,128]{1,0:T(8,128)(4,1)S(1)} %get-tuple-element.355) | copy-start | bytes 49156
  195.0 58.4 %copy-start = (f32[12,1,128,128]{2,3,1,0:T(8,128)}, f32[12,1,128,128]{2,3,1,0:T(8,128)S(1)}, u32[]{:S(2)}) copy-start(f32[12,1,128,128]{2,3,1,0:T(8,128)S(1)} %custom-call.16) | copy-start | bytes 2359300
  199.7 114.1 %all-gather.23.cloned.1.call-start = ((), (), s32[]{:S(2)}) async-start(), calls=%async_computation.15 | async-start | bytes 1966080 | tf_op jit(solution)/shard_map/all_gather | solution.py:185
  203.5 56.2 %copy-start.16 = (bf16[128,1536]{0,1:T(8,128)(2,1)}, bf16[128,1536]{0,1:T(8,128)(2,1)S(1)}, u32[]{:S(2)}) copy-start(bf16[128,1536]{0,1:T(8,128)(2,1)S(1)} %copy.185) | copy-start | bytes 1179652
  205.2 52.3 %copy-start.9 = (f32[12,128,128]{2,1,0:T(8,128)}, f32[12,128,128]{2,1,0:T(8,128)S(1)}, u32[]{:S(2)}) copy-start(f32[12,128,128]{2,1,0:T(8,128)S(1)} %fusion.105) | copy-start | bytes 2359300
  207.7 142.3 %all-gather.27.cloned.1.call-start = ((), (), s32[]{:S(2)}) async-start(), calls=%async_computation.17 | async-start | bytes 1966080 | tf_op jit(solution)/shard_map/all_gather | solution.py:188
  211.7 194.5 %all-gather.29.cloned.1.call-start = ((), (), s32[]{:S(2)}) async-start(), calls=%async_computation.18 | async-start | bytes 5898240 | tf_op jit(solution)/shard_map/all_gather | solution.py:159
  212.4 318.1 %all-gather.31.cloned.1.call-start = ((), (), s32[]{:S(2)}) async-start(), calls=%async_computation.19 | async-start | bytes 15728640 | tf_op jit(solution)/shard_map/all_gather | solution.py:161
  213.2 441.6 %all-gather.33.cloned.1.call-start = ((), (), s32[]{:S(2)}) async-start(), calls=%async_computation.20 | async-start | bytes 15728640 | tf_op jit(solution)/shard_map/all_gather | solution.py:162
  213.8 565.4 %all-gather.35.cloned.1.call-start = ((), (), s32[]{:S(2)}) async-start(), calls=%async_computation.21 | async-start | bytes 15728640 | tf_op jit(solution)/shard_map/all_gather | solution.py:163
  214.5 723.2 %reduce-scatter.37.cloned.1.call-start = ((), (), s32[]{:S(2)}) async-start(), calls=%async_computation.32 | async-start | bytes 1966080
  842.7 108.4 %reduce-scatter.39.cloned.1.call-start = ((), (), s32[]{:S(2)}) async-start(), calls=%async_computation.33 | async-start | bytes 1966080
  855.2 116.5 %reduce-scatter.43.cloned.1.call-start = ((), (), s32[]{:S(2)}) async-start(), calls=%async_computation.35 | async-start | bytes 1966080
  905.7 116.4 %reduce-scatter.21.cloned.1.call-start = ((), (), s32[]{:S(2)}) async-start(), calls=%async_computation.22 | async-start | bytes 5898240 | tf_op jit(solution)/shard_map/reduce_scatter | solution.py:299
  922.7 140.5 %reduce-scatter.29.cloned.1.call-start = ((), (), s32[]{:S(2)}) async-start(), calls=%async_computation.26 | async-start | bytes 5898240 | tf_op jit(solution)/shard_map/reduce_scatter | solution.py:314
  927.7 196.1 %reduce-scatter.23.cloned.1.call-start = ((), (), s32[]{:S(2)}) async-start(), calls=%async_computation.23 | async-start | bytes 5898240 | tf_op jit(solution)/shard_map/reduce_scatter | solution.py:302
  951.1 233.3 %reduce-scatter.25.cloned.1.call-start = ((), (), s32[]{:S(2)}) async-start(), calls=%async_computation.24 | async-start | bytes 5898240 | tf_op jit(solution)/shard_map/reduce_scatter | solution.py:305
  960.3 284.1 %reduce-scatter.27.cloned.1.call-start = ((), (), s32[]{:S(2)}) async-start(), calls=%async_computation.25 | async-start | bytes 5898240 | tf_op jit(solution)/shard_map/reduce_scatter | solution.py:308
  996.2 372.0 %reduce-scatter.31.cloned.1.call-start = ((), (), s32[]{:S(2)}) async-start(), calls=%async_computation.27 | async-start | bytes 15728640 | tf_op jit(solution)/shard_map/reduce_scatter | solution.py:320
  1004.1 488.0 %reduce-scatter.33.cloned.1.call-start = ((), (), s32[]{:S(2)}) async-start(), calls=%async_computation.28 | async-start | bytes 15728640 | tf_op jit(solution)/shard_map/reduce_scatter | solution.py:323
  1011.7 604.2 %reduce-scatter.35.cloned.1.call-start = ((), (), s32[]{:S(2)}) async-start(), calls=%async_computation.29 | async-start | bytes 15728640 | tf_op jit(solution)/shard_map/reduce_scatter | solution.py:326
  1020.1 669.1 %reduce-scatter.41.cloned.1.call-start = ((), (), s32[]{:S(2)}) async-start(), calls=%async_computation.34 | async-start | bytes 491520
  1022.1 714.8 %all-gather.39.cloned.1.call-start = ((), (), s32[]{:S(2)}) async-start(), calls=%async_computation.31 | async-start | bytes 10616832 | tf_op jit(solution)/shard_map/all_gather | solution.py:332
  1022.6 1002.1 %all-reduce.9.cloned.1.call-start = ((), (), s32[]{:S(2)}) async-start(), calls=%async_computation.36 | async-start | bytes 28311552 | tf_op jit(solution)/shard_map/psum | solution.py:335
  1630.2 58.0 %copy-start.135 = (f32[128]{0:T(128)S(1)}, f32[128]{0:T(128)}, u32[]{:S(2)}) copy-start(f32[128]{0:T(128)} %copy-done.134) | copy-start | bytes 1540
  1630.2 58.0 %copy-start.23 = (f32[128,1536]{1,0:T(8,128)S(1)}, f32[128,1536]{1,0:T(8,128)}, u32[]{:S(2)}) copy-start(f32[128,1536]{1,0:T(8,128)} %copy-done.22) | copy-start | bytes 2359300
  (137 other events, 731.7 us)
Sparse Core Ops, SparseCore 0:
  9.9 60.0 all-gather.20
  71.8 57.5 all-gather.18
  131.2 57.3 all-gather.24
  190.3 57.1 all-gather.16
  249.7 30.9 all-gather.36
  283.0 30.8 all-gather.22
  316.2 30.9 all-gather.26
  349.1 57.0 all-gather.28
  408.0 122.5 all-gather.30
  532.3 122.5 all-gather.32
  656.7 122.5 all-gather.34
  842.8 30.9 reduce-scatter.36
  877.4 30.9 reduce-scatter.38
  911.8 30.9 reduce-scatter.42
  946.1 57.0 reduce-scatter.20
  1006.1 57.0 reduce-scatter.28
  1066.7 57.0 reduce-scatter.22
  1127.2 57.0 reduce-scatter.24
  1187.3 57.0 reduce-scatter.26
  1247.4 120.7 reduce-scatter.30
  1371.3 120.7 reduce-scatter.32
  1495.2 120.7 reduce-scatter.34
  1619.3 24.5 reduce-scatter.40
  1645.4 91.4 all-gather.38
  1739.8 284.9 all-reduce.8
